TPU v7x, 32 devices: a whole 2x2x4 slice. The times are simulated.
32 devices in a mesh: seq: 4 (over y, x), fsdp: 8 (over z, core).
Axes of the slice: x: 2, y: 2, z: 4, core: 2. Of those that a mesh axis runs over, the one named last changes fastest.
Arguments:
- frames: bfloat16 [8, 2048, 1536], P('fsdp', 'seq'), may hold values from -6 to 6
- lengths: int32 [8], P('fsdp'), may hold values from 512 to 2048, as said below
- gain: float32 [1536], replicated, may hold values from 0.5 to 1.5
- w_pointwise: bfloat16 [1536, 3072], P('fsdp'), may hold values from -0.15625 to 0.15625
- w_depthwise: float32 [31, 1536], replicated, may hold values from -1 to 1
- w_output: bfloat16 [1536, 1536], P('fsdp'), may hold values from -0.15625 to 0.15625
- cotangent: bfloat16 [8, 2048, 1536], P('fsdp', 'seq'), may hold values from -6 to 6
Outputs:
- output: bfloat16 [8, 2048, 1536], P('fsdp', 'seq')
- grad_frames: bfloat16 [8, 2048, 1536], P('fsdp', 'seq')
- grad_pointwise: float32 [1536, 3072], P('fsdp')
- grad_output: float32 [1536, 1536], P('fsdp')
- grad_gain: float32 [1536], replicated
- grad_depthwise: float32 [31, 1536], replicated
Inputs may be any that keep to these rules, and one draw needn't show every extreme that they name: `lengths`: the first utterance fills all 2048 slots.
All inputs are finite; a program needn't handle non-finite values.
Results may differ from a plain program's by a relative error of at most 0.014.
Values may be sent and summed in bfloat16 or wider, within the bound.
No kernel may reach another device: no remote copies, remote signals or barrier semaphores. Data moves between devices by JAX's collectives and lax.ppermute only.
A program may use at most 128 MiB of HBM per device.

v0:
```python
import jax
import jax.numpy as jnp
from jax import lax
from jax.sharding import PartitionSpec as P

EPS = 1e-05


def extended(block, sides, width):
    for axis, dim in sides:
        count = lax.axis_size(axis)
        forward = [(i, i + 1) for i in range(count - 1)]
        backward = [(target, source) for source, target in forward]
        low = lax.ppermute(
            lax.slice_in_dim(block, block.shape[dim] - width, None, axis=dim), axis, forward
        )
        high = lax.ppermute(lax.slice_in_dim(block, 0, width, axis=dim), axis, backward)
        block = jnp.concatenate([low, block, high], axis=dim)
    return block


def rounded_term(left, right):
    term = lax.dot_general(
        left, right, (((0,), (0,)), ((), ())), preferred_element_type=jnp.float32
    )
    term = lax.optimization_barrier(term.astype(jnp.bfloat16))
    return term.astype(jnp.float32)


def on_device(frames, lengths, gain, w_pointwise, w_depthwise, w_output, cotangent):
    frame_count = frames.shape[1]
    width = frames.shape[2]
    taps = w_depthwise.shape[0]
    half_width = (taps - 1) // 2
    full_pointwise, full_output = (
        lax.all_gather(w_pointwise, "fsdp", axis=0, tiled=True),
        lax.all_gather(w_output, "fsdp", axis=0, tiled=True),
    )
    as_float = frames[0].astype(jnp.float32)
    center = jnp.mean(as_float, axis=-1, keepdims=True)
    spread = jnp.mean((as_float - center) ** 2, axis=-1, keepdims=True)
    inverse = lax.rsqrt(spread + EPS)
    normed = (as_float - center) * inverse
    lifted = (normed * gain).astype(jnp.bfloat16)
    position = lax.axis_index("seq") * frame_count + jnp.arange(frame_count, dtype=jnp.int32)
    mask = (position < lengths[0]).astype(jnp.float32)[:, None]
    joined = jnp.dot(lifted, full_pointwise, preferred_element_type=jnp.float32)
    value = joined[:, :width]
    gate_sig = jax.nn.sigmoid(joined[:, width:])
    glu = (value * gate_sig * mask).astype(jnp.bfloat16)
    glu_ext = extended(glu[None], (("seq", 1),), half_width)[0].astype(jnp.float32)
    conv = jnp.zeros((frame_count, width), jnp.float32)
    for offset in range(taps):
        conv = conv + w_depthwise[offset] * glu_ext[offset : offset + frame_count]
    conv_sig = jax.nn.sigmoid(conv)
    swished = (conv * conv_sig).astype(jnp.bfloat16)
    branch = jnp.dot(swished, full_output, preferred_element_type=jnp.float32)
    output = (as_float + branch).astype(jnp.bfloat16)
    branch_grad = (cotangent[0].astype(jnp.float32) * mask).astype(jnp.bfloat16)
    swish_grad = lax.dot_general(
        branch_grad, full_output, (((1,), (1,)), ((), ())), preferred_element_type=jnp.float32
    )
    conv_grad = (swish_grad * conv_sig * (1.0 + conv * (1.0 - conv_sig))).astype(jnp.bfloat16)
    grad_ext = extended(conv_grad[None], (("seq", 1),), half_width)[0].astype(jnp.float32)
    conv_grad_f = conv_grad.astype(jnp.float32)
    glu_grad = jnp.zeros((frame_count, width), jnp.float32)
    tap_rows = []
    for offset in range(taps):
        back = taps - 1 - offset
        glu_grad = glu_grad + w_depthwise[offset] * grad_ext[back : back + frame_count]
        tap_rows.append(jnp.sum(conv_grad_f * glu_ext[offset : offset + frame_count], axis=0))
    glu_grad = glu_grad * mask
    joined_grad = jnp.concatenate(
        [glu_grad * gate_sig, glu_grad * value * gate_sig * (1.0 - gate_sig)], axis=-1
    ).astype(jnp.bfloat16)
    lifted_grad = lax.dot_general(
        joined_grad, full_pointwise, (((1,), (1,)), ((), ())), preferred_element_type=jnp.float32
    )
    gain_term = jnp.sum(lifted_grad * normed, axis=0)
    grad_gain, grad_depthwise = lax.psum((gain_term, jnp.stack(tap_rows, axis=0)), ("seq", "fsdp"))
    scaled = lifted_grad * gain
    norm_grad = inverse * (
        scaled
        - jnp.mean(scaled, axis=-1, keepdims=True)
        - normed * jnp.mean(scaled * normed, axis=-1, keepdims=True)
    )
    grad_frames = (cotangent[0].astype(jnp.float32) + norm_grad).astype(jnp.bfloat16)
    term_pointwise = rounded_term(lifted, joined_grad)
    term_output = rounded_term(swished, branch_grad)
    owned = (
        lax.psum_scatter(
            term_pointwise.astype(jnp.bfloat16), "fsdp", scatter_dimension=0, tiled=True
        ).astype(jnp.float32),
        lax.psum_scatter(
            term_output.astype(jnp.bfloat16), "fsdp", scatter_dimension=0, tiled=True
        ).astype(jnp.float32),
    )
    grad_pointwise, grad_output = (
        lax.psum(owned[0].astype(jnp.bfloat16), "seq").astype(jnp.float32),
        lax.psum(owned[1].astype(jnp.bfloat16), "seq").astype(jnp.float32),
    )
    return (output[None], grad_frames[None], grad_pointwise, grad_output, grad_gain, grad_depthwise)


def solution(mesh):
    in_specs = (
        P("fsdp", "seq", None),
        P("fsdp"),
        P(),
        P("fsdp", None),
        P(),
        P("fsdp", None),
        P("fsdp", "seq", None),
    )
    out_specs = (
        P("fsdp", "seq", None),
        P("fsdp", "seq", None),
        P("fsdp", None),
        P("fsdp", None),
        P(),
        P(),
    )
    return jax.shard_map(
        on_device, mesh=mesh, in_specs=in_specs, out_specs=out_specs, check_vma=False
    )
```

profile of v0, /device:TPU:10, one launch (start us, length us, event | category | flops | bytes accessed | tf_op | source)
XLA Modules:
  0.0 515.2 jit_solution(6867970955985143212)
XLA Ops:
  7.2 0.0 all-gather.3.cloned.1.call-start
  7.2 0.7 all-gather.3.cloned.1.call-update
  7.9 0.0 all-gather.5.cloned.1.call-start
  8.0 0.7 all-gather.5.cloned.1.call-update
  8.7 0.0 reduce-scatter.5.cloned.1.call-start
  9.4 1.7 convert_reduce_fusion
  11.1 0.5 fusion.14
  11.7 0.3 slice_reduce_fusion.30
  12.0 87.0 %all-gather.3.cloned.1.call-done = bf16[1536,3072]{1,0:T(8,128)(2,1)} async-done(((bf16[192,3072]{1,0:T(8,128)(2,1)}), bf16[1536,3072]{1,0:T(8,128)(2,1)}) %all-gather.3.cloned.1.call-update) | async-done | bytes 9437200 | tf_op jit(solution)/shard_map/all_gather | solution.py:36
  99.1 7.7 %fusion.125 = f32[512,3072]{1,0:T(8,128)S(1)} fusion(bf16[1536,3072]{1,0:T(8,128)(2,1)} %all-gather.3.cloned.1.call-done, bf16[1,512,1536]{2,1,0:T(8,128)(2,1)S(1)} %copy-done.1, f32[1536]{0:T(1024)S(1)} %copy-done.41, f32[512]{0:T(512)S(1)} %add_rsqrt_fusion, f32[512]{0:T(512)S(1)} %broadcast_multiply_fusion.2), kind=kOutput, calls=%fused_computation.269 | convolution fusion | flops 4835770368 | bytes 17311744 | tf_op jit(solution)/shard_map/dot_general | solution.py:47
  106.8 0.8 fusion.117
  107.6 1.8 copy-done
  109.5 3.4 collective-permute-start
  112.9 2.5 collective-permute-start.1
  115.3 0.2 slice_reduce_fusion.29
  115.6 4.1 collective-permute-done.1
  119.7 0.5 maximum_convert_fusion
  120.2 12.0 %multiply_add_fusion = f32[512,1536]{1,0:T(8,128)S(1)} fusion(f32[1,542,1536]{2,1,0:T(8,128)S(1)} %maximum_convert_fusion, f32[1536]{0:T(1024)S(1)} %get-tuple-element.69, f32[1536]{0:T(1024)S(1)} %get-tuple-element.70, f32[1536]{0:T(1024)S(1)} %get-tuple-element.41, f32[1536]{0:T(1024)S(1)} %get-tuple-element.42, f32[1536]{0:T(1024)S(1)} %get-tuple-element.43, ...), kind=kLoop, calls=%fused_computation.219 | loop fusion | flops 47972352 | bytes 100853760 | tf_op jit(solution)/shard_map/add | solution.py:54
  132.3 1.7 copy-done.4
  134.0 4.8 convolution_convert_fusion.1
  138.8 0.0 reduce-scatter.5.cloned.1.call-update
  138.9 0.0 reduce-scatter.3.cloned.1.call-start
  138.9 13.0 %all-gather.5.cloned.1.call-done = bf16[1536,1536]{1,0:T(8,128)(2,1)} async-done(((bf16[192,1536]{1,0:T(8,128)(2,1)}), bf16[1536,1536]{1,0:T(8,128)(2,1)}) %all-gather.5.cloned.1.call-update) | async-done | bytes 4718608 | tf_op jit(solution)/shard_map/all_gather | solution.py:37
  151.9 12.6 %fusion.46 = (f32[1536]{0:T(1024)}, f32[1536]{0:T(1024)}, f32[1536]{0:T(1024)}, f32[1536]{0:T(1024)}, f32[1536]{0:T(1024)}, /*index=5*/f32[1536]{0:T(1024)}, f32...) fusion(f32[1,542,1536]{2,1,0:T(8,128)S(1)} %maximum_convert_fus, ...), kind=kOutput, calls=%fused_computation.84 | convolution fusion | flops 2446569984 | bytes 51986432 | tf_op jit(solution)/shard_map/dot_general | solution.py:60
  164.5 0.9 fusion.128
  165.4 3.4 collective-permute-start.2
  168.8 2.6 collective-permute-start.3
  171.5 4.2 collective-permute-done.3
  175.7 2.1 maximum_convert_fusion.1
  177.8 14.4 %multiply_convert_fusion.1 = (bf16[512,1536]{1,0:T(8,128)(2,1)S(1)}, f32[512,1536]{1,0:T(8,128)S(1)}) fusion(f32[512,3072]{1,0:T(8,128)} %copy-done, f32[512]{0:T(512)S(1)} %copy-done.25, f32[1,542,1536]{2,1,0:T(8,128)S(1)} %maximum_convert_fusion.1, f32[1536]{0:T(1024)S(1)} %copy-done.20, f32[1536]{0:T(1024)S(1)} %copy-done.22, ...), kind=kLoop, calls=%fused_computation.216 | loop fusion | flops 52690944 | bytes 105574400 | tf_op jit(solution)/shard_map/convert.1
  192.3 1.3 multiply_convert_fusion
  193.6 1.1 copy-done.7
  194.7 8.1 %convolution_convert_fusion = bf16[1536,3072]{1,0:T(8,128)(2,1)} fusion(bf16[512,1536]{1,0:T(8,128)(2,1)S(1)} %multiply_convert_fusion, bf16[512,1536]{1,0:T(8,128)(2,1)S(1)} %get-tuple-element.73, bf16[1,512,1536]{2,1,0:T(8,128)(2,1)S(1)} %copy-done.2, f32[1536]{0:T(1024)S(1)} %copy-done.42, f32[512]{0:T(512)S(1)} %copy-done.44, f32[512]{0:T(512)S(1)} %copy-done.27), kind=kOutput, calls=%fused_computation.31 | convolution fusion | flops 4846780416 | bytes 14166016 | tf_op jit(solution)/shard_map/dot_general | solution.py:23
  202.8 0.0 reduce-scatter.3.cloned.1.call-update
  202.8 0.0 all-reduce.6.cloned.1.call-start
  202.9 3.9 reduce-scatter.5.cloned.1.call-done
  206.7 100.1 %reduce-scatter.3.cloned.1.call-done = bf16[192,3072]{1,0:T(8,128)(2,1)} async-done(((bf16[1536,3072]{1,0:T(8,128)(2,1)}), bf16[192,3072]{1,0:T(8,128)(2,1)}) %reduce-scatter.3.cloned.1.call-update) | async-done | bytes 1179664 | tf_op jit(solution)/shard_map/reduce_scatter | solution.py:91
  307.0 0.3 all-reduce.4.cloned.1.call-start
  307.2 8.3 %fusion.47 = (f32[1536]{0:T(1024)S(1)}, f32[1536]{0:T(1024)S(1)}, f32[1536]{0:T(1024)S(1)}, f32[1536]{0:T(1024)S(1)}, f32[1536]{0:T(1024)S(1)}, /*index=5*/f32[1...) fusion(bf16[512,1536]{1,0:T(8,128)(2,1)} %get-tuple-element.80,, ...), kind=kLoop, calls=%fused_computation.85 | loop fusion | flops 29070336 | bytes 58306560 | tf_op jit(solution)/shard_map/reduce_sum | solution.py:71
  316.1 2.8 stack.127
  318.9 7.7 %fusion.115 = bf16[1,512,1536]{2,1,0:T(8,128)(2,1)} fusion(bf16[1536,1536]{1,0:T(8,128)(2,1)} %all-gather.5.cloned.1.call-done, bf16[1,512,1536]{2,1,0:T(8,128)(2,1)} %param.7, f32[512,1536]{1,0:T(8,128)} %copy-done.4), kind=kOutput, calls=%fused_computation.224 | convolution fusion | flops 2422210560 | bytes 11010048 | tf_op jit(solution)/shard_map/dot_general | solution.py:57
  326.6 8.6 %fusion.13 = (f32[1536]{0:T(1024)S(1)}, f32[512]{0:T(512)S(1)}, f32[512]{0:T(512)S(1)}, f32[512,1536]{1,0:T(8,128)S(1)}) fusion(bf16[1,512,1536]{2,1,0:T(8,128)(2,1)S(1)} %copy-done.3, f32[512]{0:T(512)S(1)} %copy-done.44, f32[512]{0:T(512)S(1)} %copy-done.27, f32[1536]{0:T(1024)S(1)} %copy-done.42, bf16[1536,3072]{1,0:T(8,128)(2,1)} %all-gather.3.cloned.1.call-done, ...), kind=kOutput, calls=%fused_computation.51 | convolution fusion | flops 4845204992 | bytes 17321984 | tf_op jit(solution)/shard_map/dot_general | solution.py:76
  335.2 2.4 fusion.118
  337.7 43.1 %psum.30 = f32[1536]{0:T(1024)} all-reduce(f32[1536]{0:T(1024)S(1)} %get-tuple-element.37), channel_id=1, replica_groups=mesh['seq'=4,'fsdp'=8] {'seq','fsdp'}, use_global_device_ids=true, to_apply=%region_9.0 | all-reduce | flops 1536 | bytes 12288 | tf_op jit(solution)/shard_map/psum | solution.py:80
  380.7 3.0 convert_element_type.88
  383.7 1.1 convert_element_type.90
  384.9 121.9 %all-reduce.4.cloned.1.call-done = f32[31,1536]{1,0:T(8,128)} async-done(((f32[31,1536]{1,0:T(8,128)}), f32[31,1536]{1,0:T(8,128)}) %all-reduce.4.cloned.1.call-update) | async-done | bytes 190480 | tf_op jit(solution)/shard_map/psum | solution.py:80
  506.8 1.6 copy.17
  (133 shorter events, 0.5 us)
Async XLA Ops:
  7.2 3.9 copy-start.1
  7.2 4.5 copy-start.12
  7.2 91.9 %copy-start.41 = (f32[1536]{0:T(1024)S(1)}, f32[1536]{0:T(1024)}, u32[]{:S(2)}) copy-start(f32[1536]{0:T(1024)} %param.9) | copy-start | bytes 18436
  7.2 91.9 %all-gather.3.cloned.1.call-start = ((), (), s32[]{:S(2)}) async-start(), calls=%async_computation.2 | async-start | bytes 10616832 | tf_op jit(solution)/shard_map/all_gather | solution.py:36
  7.9 144.0 %all-gather.5.cloned.1.call-start = ((), (), s32[]{:S(2)}) async-start(), calls=%async_computation.3 | async-start | bytes 5308416 | tf_op jit(solution)/shard_map/all_gather | solution.py:37
  8.7 198.1 %reduce-scatter.5.cloned.1.call-start = ((), (), s32[]{:S(2)}) async-start(), calls=%async_computation.5 | async-start | bytes 5308416 | tf_op jit(solution)/shard_map/reduce_scatter | solution.py:94
  11.1 95.6 %copy-start.26 = (f32[512]{0:T(512)}, f32[512]{0:T(512)S(1)}, u32[]{:S(2)}) copy-start(f32[512]{0:T(512)S(1)} %broadcast_multiply_fusion.2) | copy-start | bytes 6148
  11.7 95.1 %copy-start.43 = (f32[512]{0:T(512)}, f32[512]{0:T(512)S(1)}, u32[]{:S(2)}) copy-start(f32[512]{0:T(512)S(1)} %add_rsqrt_fusion) | copy-start | bytes 6148
  12.0 94.7 %copy-start.23 = (f32[512]{0:T(512)}, f32[512]{0:T(512)S(1)}, u32[]{:S(2)}) copy-start(f32[512]{0:T(512)S(1)} %fusion.121) | copy-start | bytes 6148
  109.5 6.1 %collective-permute-start = (bf16[1,15,1536]{2,1,0:T(8,128)(2,1)S(1)}, bf16[1,15,1536]{2,1,0:T(8,128)(2,1)S(1)}, u32[]{:S(2)}, u32[]{:S(2)}) collective-permute-start(bf16[1,15,1536]{2,1,0:T(8,128)(2,1)S(1)} %get-tuple-element.77), channel_id=1, source_target_pairs={{0,8},{8,16},{16,24},{1,9},{9,17},{17,25},{2,10},{10,18},{18,26},{... | collective-permute-start | bytes 138248 | tf_op jit(solution)/shard_map/ppermute | solution.py:14
  112.9 6.9 %collective-permute-start.1 = (bf16[1,15,1536]{2,1,0:T(8,128)(2,1)S(1)}, bf16[1,15,1536]{2,1,0:T(8,128)(2,1)S(1)}, u32[]{:S(2)}, u32[]{:S(2)}) collective-permute-start(bf16[1,15,1536]{2,1,0:T(8,128)(2,1)S(1)} %get-tuple-element.78), channel_id=1, source_target_pairs={{8,0},{16,8},{24,16},{9,1},{17,9},{25,17},{10,2},{18,10},{26,18},{... | collective-permute-start | bytes 138248 | tf_op jit(solution)/shard_map/ppermute | solution.py:17
  115.5 16.7 %copy-start.13 = (f32[1536]{0:T(1024)}, f32[1536]{0:T(1024)S(1)}, u32[]{:S(2)}) copy-start(f32[1536]{0:T(1024)S(1)} %get-tuple-element.66) | copy-start | bytes 18436
  115.5 16.7 %copy-start.15 = (f32[1536]{0:T(1024)}, f32[1536]{0:T(1024)S(1)}, u32[]{:S(2)}) copy-start(f32[1536]{0:T(1024)S(1)} %get-tuple-element.67) | copy-start | bytes 18436
  115.5 16.7 %copy-start.17 = (f32[1536]{0:T(1024)}, f32[1536]{0:T(1024)S(1)}, u32[]{:S(2)}) copy-start(f32[1536]{0:T(1024)S(1)} %get-tuple-element.68) | copy-start | bytes 18436
  115.6 16.7 %copy-start.19 = (f32[1536]{0:T(1024)}, f32[1536]{0:T(1024)S(1)}, u32[]{:S(2)}) copy-start(f32[1536]{0:T(1024)S(1)} %get-tuple-element.69) | copy-start | bytes 18436
  115.6 16.7 %copy-start.21 = (f32[1536]{0:T(1024)}, f32[1536]{0:T(1024)S(1)}, u32[]{:S(2)}) copy-start(f32[1536]{0:T(1024)S(1)} %get-tuple-element.70) | copy-start | bytes 18436
  120.2 13.8 %copy-start.5 = (bf16[1,512,1536]{2,1,0:T(8,128)(2,1)S(1)}, bf16[1,512,1536]{2,1,0:T(8,128)(2,1)}, u32[]{:S(2)}) copy-start(bf16[1,512,1536]{2,1,0:T(8,128)(2,1)} %param.13) | copy-start | bytes 4718596
  120.2 13.8 %copy-start.24 = (f32[512]{0:T(512)S(1)}, f32[512]{0:T(512)}, u32[]{:S(2)}) copy-start(f32[512]{0:T(512)} %copy-done.23) | copy-start | bytes 6148
  138.9 167.9 %reduce-scatter.3.cloned.1.call-start = ((), (), s32[]{:S(2)}) async-start(), calls=%async_computation.4 | async-start | bytes 10616832 | tf_op jit(solution)/shard_map/reduce_scatter | solution.py:91
  164.5 13.3 %copy-start.14 = (f32[1536]{0:T(1024)S(1)}, f32[1536]{0:T(1024)}, u32[]{:S(2)}) copy-start(f32[1536]{0:T(1024)} %copy-done.13) | copy-start | bytes 18436
  164.5 13.3 %copy-start.16 = (f32[1536]{0:T(1024)S(1)}, f32[1536]{0:T(1024)}, u32[]{:S(2)}) copy-start(f32[1536]{0:T(1024)} %copy-done.15) | copy-start | bytes 18436
  164.5 13.3 %copy-start.18 = (f32[1536]{0:T(1024)S(1)}, f32[1536]{0:T(1024)}, u32[]{:S(2)}) copy-start(f32[1536]{0:T(1024)} %copy-done.17) | copy-start | bytes 18436
  164.5 13.3 %copy-start.20 = (f32[1536]{0:T(1024)S(1)}, f32[1536]{0:T(1024)}, u32[]{:S(2)}) copy-start(f32[1536]{0:T(1024)} %copy-done.19) | copy-start | bytes 18436
  164.5 13.3 %copy-start.22 = (f32[1536]{0:T(1024)S(1)}, f32[1536]{0:T(1024)}, u32[]{:S(2)}) copy-start(f32[1536]{0:T(1024)} %copy-done.21) | copy-start | bytes 18436
  164.5 13.3 %copy-start.25 = (f32[512]{0:T(512)S(1)}, f32[512]{0:T(512)}, u32[]{:S(2)}) copy-start(f32[512]{0:T(512)} %copy-done.23) | copy-start | bytes 6148
  165.4 6.0 %collective-permute-start.2 = (bf16[1,15,1536]{2,1,0:T(8,128)(2,1)S(1)}, bf16[1,15,1536]{2,1,0:T(8,128)(2,1)S(1)}, u32[]{:S(2)}, u32[]{:S(2)}) collective-permute-start(bf16[1,15,1536]{2,1,0:T(8,128)(2,1)S(1)} %get-tuple-element.75), channel_id=1, source_target_pairs={{0,8},{8,16},{16,24},{1,9},{9,17},{17,25},{2,10},{10,18},{18,26},{... | collective-permute-start | bytes 138248 | tf_op jit(solution)/shard_map/ppermute | solution.py:14
  168.8 6.9 %collective-permute-start.3 = (bf16[1,15,1536]{2,1,0:T(8,128)(2,1)S(1)}, bf16[1,15,1536]{2,1,0:T(8,128)(2,1)S(1)}, u32[]{:S(2)}, u32[]{:S(2)}) collective-permute-start(bf16[1,15,1536]{2,1,0:T(8,128)(2,1)S(1)} %get-tuple-element.76), channel_id=1, source_target_pairs={{8,0},{16,8},{24,16},{9,1},{17,9},{25,17},{10,2},{18,10},{26,18},{... | collective-permute-start | bytes 138248 | tf_op jit(solution)/shard_map/ppermute | solution.py:17
  175.7 16.5 %slice-start = ((s8[6291456]{0:T(1024)(128)(4,1)}), s8[4194304]{0:T(1024)(128)(4,1)S(1)}, s32[]{:S(2)}) async-start(s8[6291456]{0:T(1024)(128)(4,1)} %bitcast.526), calls=%async_computation.8 | async-start | bytes 8388608
  177.8 14.4 %slice-start.1 = ((s8[6291456]{0:T(1024)(128)(4,1)}), s8[2097152]{0:T(1024)(128)(4,1)S(1)}, s32[]{:S(2)}) async-start(s8[6291456]{0:T(1024)(128)(4,1)} %bitcast.526), calls=%async_computation.9 | async-start | bytes 4194304
  202.8 177.9 %all-reduce.6.cloned.1.call-start = ((), (), s32[]{:S(2)}) async-start(), calls=%async_computation.7 | async-start | bytes 3538944 | tf_op jit(solution)/shard_map/psum | solution.py:99
  306.8 8.7 %copy-start.40 = (f32[1536]{0:T(1024)S(1)}, f32[1536]{0:T(1024)}, u32[]{:S(2)}) copy-start(f32[1536]{0:T(1024)} %get-tuple-element.24) | copy-start | bytes 18436
  306.8 8.7 %copy-start.39 = (f32[1536]{0:T(1024)S(1)}, f32[1536]{0:T(1024)}, u32[]{:S(2)}) copy-start(f32[1536]{0:T(1024)} %get-tuple-element.25) | copy-start | bytes 18436
  306.8 8.8 %copy-start.38 = (f32[1536]{0:T(1024)S(1)}, f32[1536]{0:T(1024)}, u32[]{:S(2)}) copy-start(f32[1536]{0:T(1024)} %get-tuple-element.26) | copy-start | bytes 18436
  306.9 8.8 %copy-start.37 = (f32[1536]{0:T(1024)S(1)}, f32[1536]{0:T(1024)}, u32[]{:S(2)}) copy-start(f32[1536]{0:T(1024)} %get-tuple-element.27) | copy-start | bytes 18436
  306.9 8.8 %copy-start.36 = (f32[1536]{0:T(1024)S(1)}, f32[1536]{0:T(1024)}, u32[]{:S(2)}) copy-start(f32[1536]{0:T(1024)} %get-tuple-element.28) | copy-start | bytes 18436
  306.9 8.8 %copy-start.35 = (f32[1536]{0:T(1024)S(1)}, f32[1536]{0:T(1024)}, u32[]{:S(2)}) copy-start(f32[1536]{0:T(1024)} %get-tuple-element.29) | copy-start | bytes 18436
  306.9 8.8 %copy-start.34 = (f32[1536]{0:T(1024)S(1)}, f32[1536]{0:T(1024)}, u32[]{:S(2)}) copy-start(f32[1536]{0:T(1024)} %get-tuple-element.30) | copy-start | bytes 18436
  306.9 8.8 %copy-start.33 = (f32[1536]{0:T(1024)S(1)}, f32[1536]{0:T(1024)}, u32[]{:S(2)}) copy-start(f32[1536]{0:T(1024)} %get-tuple-element.31) | copy-start | bytes 18436
  306.9 8.8 %copy-start.32 = (f32[1536]{0:T(1024)S(1)}, f32[1536]{0:T(1024)}, u32[]{:S(2)}) copy-start(f32[1536]{0:T(1024)} %get-tuple-element.32) | copy-start | bytes 18436
  306.9 8.9 %copy-start.31 = (f32[1536]{0:T(1024)S(1)}, f32[1536]{0:T(1024)}, u32[]{:S(2)}) copy-start(f32[1536]{0:T(1024)} %get-tuple-element.33) | copy-start | bytes 18436
  306.9 8.9 %copy-start.30 = (f32[1536]{0:T(1024)S(1)}, f32[1536]{0:T(1024)}, u32[]{:S(2)}) copy-start(f32[1536]{0:T(1024)} %get-tuple-element.34) | copy-start | bytes 18436
  306.9 8.9 %copy-start.29 = (f32[1536]{0:T(1024)S(1)}, f32[1536]{0:T(1024)}, u32[]{:S(2)}) copy-start(f32[1536]{0:T(1024)} %get-tuple-element.35) | copy-start | bytes 18436
  307.0 8.9 %copy-start.28 = (f32[1536]{0:T(1024)S(1)}, f32[1536]{0:T(1024)}, u32[]{:S(2)}) copy-start(f32[1536]{0:T(1024)} %get-tuple-element.36) | copy-start | bytes 18436
  307.0 199.8 %all-reduce.4.cloned.1.call-start = ((), (), s32[]{:S(2)}) async-start(), calls=%async_computation.6 | async-start | bytes 393216 | tf_op jit(solution)/shard_map/psum | solution.py:80
  318.9 7.7 %copy-start.3 = (bf16[1,512,1536]{2,1,0:T(8,128)(2,1)S(1)}, bf16[1,512,1536]{2,1,0:T(8,128)(2,1)}, u32[]{:S(2)}) copy-start(bf16[1,512,1536]{2,1,0:T(8,128)(2,1)} %param.7) | copy-start | bytes 4718596
  318.9 7.7 %copy-start.8 = (bf16[512,1536]{1,0:T(8,128)(2,1)S(1)}, bf16[512,1536]{1,0:T(8,128)(2,1)}, u32[]{:S(2)}) copy-start(bf16[512,1536]{1,0:T(8,128)(2,1)} %copy-done.7) | copy-start | bytes 4718596
  318.9 7.7 %copy-start.10 = (bf16[512,1536]{1,0:T(8,128)(2,1)S(1)}, bf16[512,1536]{1,0:T(8,128)(2,1)}, u32[]{:S(2)}) copy-start(bf16[512,1536]{1,0:T(8,128)(2,1)} %copy-done.9) | copy-start | bytes 4718596
  326.6 8.6 %copy-start.6 = (bf16[1,512,1536]{2,1,0:T(8,128)(2,1)S(1)}, bf16[1,512,1536]{2,1,0:T(8,128)(2,1)}, u32[]{:S(2)}) copy-start(bf16[1,512,1536]{2,1,0:T(8,128)(2,1)} %param.13) | copy-start | bytes 4718596
  (9 other events, 19.9 us)
Sparse Core Ops, SparseCore 0:
  9.7 89.3 all-gather.2
  100.7 51.1 all-gather.4
  154.2 52.4 reduce-scatter.4
  208.9 97.8 reduce-scatter.2
  309.9 65.7 all-reduce.5
  381.6 125.0 all-reduce.3
where the time goes:
time: 516 us; the launch traced here: 515 us
  waiting for transfers between devices  336 us (65%)
  matrix products  49.4 us (10%)
  other arithmetic  48.1 us (9%)
  blocking collectives  43.1 us (8%)
  between operations  15.8 us (3%)
  starting transfers between devices  12.3 us (2%)
  local copies, waits for them, and re-layouts  10.9 us (2%)
    psum x1, waiting for transfers between devices, on_device(): lax.psum((gain_term, jnp.stack(tap_rows, axis=0)), ('seq', 'fsdp'))  122 us
    reduce_scatter x1, waiting for transfers between devices, on_device(): lax.psum_scatter(term_pointwise.astype(jnp.bfloat16), 'fsdp', scatter_dim...  100 us
    all_gather x1, waiting for transfers between devices, on_device(): lax.all_gather(w_pointwise, 'fsdp', axis=0, tiled=True)  87 us
    psum x1, blocking collectives, on_device(): lax.psum((gain_term, jnp.stack(tap_rows, axis=0)), ('seq', 'fsdp'))  43.1 us
    another operation x2, other arithmetic  15.6 us
    all_gather x1, waiting for transfers between devices, on_device(): lax.all_gather(w_output, 'fsdp', axis=0, tiled=True)  13 us
    dot_general x2, matrix products, rounded_term(): lax.dot_general(left, right, (((0,), (0,)), ((), ())), preferred_element_...  12.9 us
    dot_general x1, matrix products, on_device(): lax.dot_general(branch_grad, full_output, (((1,), (1,)), ((), ())), prefe...  12.6 us
  transfers between devices with their start and end apart: 10, of which 7 were waited for; matrix products, arithmetic and copies ran while one was open for 20% of the time, Pallas kernels for 0%

commit v1 on v0

--- a/solution.py
+++ b/solution.py
@@ -77,7 +77,9 @@
         joined_grad, full_pointwise, (((1,), (1,)), ((), ())), preferred_element_type=jnp.float32
     )
     gain_term = jnp.sum(lifted_grad * normed, axis=0)
-    grad_gain, grad_depthwise = lax.psum((gain_term, jnp.stack(tap_rows, axis=0)), ("seq", "fsdp"))
+    grad_gain, grad_depthwise = lax.psum(
+        lax.psum((gain_term, jnp.stack(tap_rows, axis=0)), "fsdp"), "seq"
+    )
     scaled = lifted_grad * gain
     norm_grad = inverse * (
         scaled

time: 516 us -> 488 us (0.946)
  blocking collectives: 43.1 us -> 20.1 us
  waiting for transfers between devices: 336 us -> 325 us
    psum x1, waiting for transfers between devices: 0.01 us -> 43.6 us  [on_device(): lax.psum(owned[0].astype(jnp.bfloat16), 'seq').astype(jnp.float32)]
    psum x1 -> x2, waiting for transfers between devices: 122 us -> 80 us  [the longest x1 41.5 us: on_device(): lax.psum(lax.psum((gain_term, jnp.stack(tap_rows, axis=0)), 'fsdp'), 'seq')]
    psum x1 -> x2, blocking collectives: 43.1 us -> 20.1 us  [the longest x1 11.3 us: on_device(): lax.psum((gain_term, jnp.stack(tap_rows, axis=0)), 'fsdp')]
    reduce_scatter x1, waiting for transfers between devices: 100 us -> 92 us  [on_device(): lax.psum_scatter(term_pointwise.astype(jnp.bfloat16), 'fsdp', scatter_dim...]
  transfers between devices with their start and end apart: 10 -> 11, of which waited for: 7 -> 8; matrix products, arithmetic and copies ran while one was open for 20% -> 22% of each run, Pallas kernels for 0% -> 0%
where the time goes in v1:
time: 488 us; the launch traced here: 486 us
  waiting for transfers between devices  325 us (67%)
  matrix products  51.9 us (11%)
  other arithmetic  50 us (10%)
  blocking collectives  20.1 us (4%)
  between operations  15.8 us (3%)
  starting transfers between devices  12.4 us (3%)
  local copies, waits for them, and re-layouts  10.9 us (2%)
    reduce_scatter x1, waiting for transfers between devices, on_device(): lax.psum_scatter(term_pointwise.astype(jnp.bfloat16), 'fsdp', scatter_dim...  92 us
    all_gather x1, waiting for transfers between devices, on_device(): lax.all_gather(w_pointwise, 'fsdp', axis=0, tiled=True)  87 us
    psum x1, waiting for transfers between devices, on_device(): lax.psum(owned[0].astype(jnp.bfloat16), 'seq').astype(jnp.float32)  43.6 us
    psum x1, waiting for transfers between devices, on_device(): lax.psum(lax.psum((gain_term, jnp.stack(tap_rows, axis=0)), 'fsdp'), 'seq')  41.5 us
    psum x1, waiting for transfers between devices, on_device(): lax.psum((gain_term, jnp.stack(tap_rows, axis=0)), 'fsdp')  38.5 us
    another operation x2, other arithmetic  15.6 us
    all_gather x1, waiting for transfers between devices, on_device(): lax.all_gather(w_output, 'fsdp', axis=0, tiled=True)  13 us
    dot_general x2, matrix products, rounded_term(): lax.dot_general(left, right, (((0,), (0,)), ((), ())), preferred_element_...  12.9 us
  transfers between devices with their start and end apart: 11, of which 8 were waited for; matrix products, arithmetic and copies ran while one was open for 22% of the time, Pallas kernels for 0%

profile of v1, /device:TPU:10, one launch (start us, length us, event | category | flops | bytes accessed | tf_op | source)
XLA Modules:
  0.0 486.5 jit_solution(10289992672641010439)
XLA Ops:
  7.2 0.7 all-gather.3.cloned.1.call-update
  7.9 0.0 all-gather.5.cloned.1.call-start
  8.0 0.7 all-gather.5.cloned.1.call-update
  8.7 0.0 reduce-scatter.5.cloned.1.call-start
  9.4 1.7 convert_reduce_fusion
  11.1 0.5 fusion.14
  11.7 0.3 slice_reduce_fusion.30
  12.0 87.0 %all-gather.3.cloned.1.call-done = bf16[1536,3072]{1,0:T(8,128)(2,1)} async-done(((bf16[192,3072]{1,0:T(8,128)(2,1)}), bf16[1536,3072]{1,0:T(8,128)(2,1)}) %all-gather.3.cloned.1.call-update) | async-done | bytes 9437200 | tf_op jit(solution)/shard_map/all_gather | solution.py:36
  99.1 7.7 %fusion.125 = f32[512,3072]{1,0:T(8,128)S(1)} fusion(bf16[1536,3072]{1,0:T(8,128)(2,1)} %all-gather.3.cloned.1.call-done, bf16[1,512,1536]{2,1,0:T(8,128)(2,1)S(1)} %copy-done.1, f32[1536]{0:T(1024)S(1)} %copy-done.41, f32[512]{0:T(512)S(1)} %add_rsqrt_fusion, f32[512]{0:T(512)S(1)} %broadcast_multiply_fusion.2), kind=kOutput, calls=%fused_computation.269 | convolution fusion | flops 4835770368 | bytes 17311744 | tf_op jit(solution)/shard_map/dot_general | solution.py:47
  106.8 0.8 fusion.117
  107.6 1.8 copy-done
  109.5 3.4 collective-permute-start
  112.9 2.5 collective-permute-start.1
  115.3 0.2 slice_reduce_fusion.29
  115.6 4.1 collective-permute-done.1
  119.7 0.5 maximum_convert_fusion
  120.2 12.0 %multiply_add_fusion = f32[512,1536]{1,0:T(8,128)S(1)} fusion(f32[1,542,1536]{2,1,0:T(8,128)S(1)} %maximum_convert_fusion, f32[1536]{0:T(1024)S(1)} %get-tuple-element.69, f32[1536]{0:T(1024)S(1)} %get-tuple-element.70, f32[1536]{0:T(1024)S(1)} %get-tuple-element.41, f32[1536]{0:T(1024)S(1)} %get-tuple-element.42, f32[1536]{0:T(1024)S(1)} %get-tuple-element.43, ...), kind=kLoop, calls=%fused_computation.219 | loop fusion | flops 47972352 | bytes 100853760 | tf_op jit(solution)/shard_map/add | solution.py:54
  132.3 1.7 copy-done.4
  134.0 4.8 convolution_convert_fusion.1
  138.9 0.0 reduce-scatter.3.cloned.1.call-start
  138.9 13.0 %all-gather.5.cloned.1.call-done = bf16[1536,1536]{1,0:T(8,128)(2,1)} async-done(((bf16[192,1536]{1,0:T(8,128)(2,1)}), bf16[1536,1536]{1,0:T(8,128)(2,1)}) %all-gather.5.cloned.1.call-update) | async-done | bytes 4718608 | tf_op jit(solution)/shard_map/all_gather | solution.py:37
  151.9 12.6 %fusion.46 = (f32[1536]{0:T(1024)}, f32[1536]{0:T(1024)}, f32[1536]{0:T(1024)}, f32[1536]{0:T(1024)}, f32[1536]{0:T(1024)}, /*index=5*/f32[1536]{0:T(1024)}, f32...) fusion(f32[1,542,1536]{2,1,0:T(8,128)S(1)} %maximum_convert_fus, ...), kind=kOutput, calls=%fused_computation.84 | convolution fusion | flops 2446569984 | bytes 51986432 | tf_op jit(solution)/shard_map/dot_general | solution.py:60
  164.5 0.9 fusion.128
  165.4 3.4 collective-permute-start.2
  168.8 2.6 collective-permute-start.3
  171.5 4.2 collective-permute-done.3
  175.7 2.1 maximum_convert_fusion.1
  177.8 14.4 %multiply_convert_fusion.1 = (bf16[512,1536]{1,0:T(8,128)(2,1)S(1)}, f32[512,1536]{1,0:T(8,128)S(1)}) fusion(f32[512,3072]{1,0:T(8,128)} %copy-done, f32[512]{0:T(512)S(1)} %copy-done.25, f32[1,542,1536]{2,1,0:T(8,128)S(1)} %maximum_convert_fusion.1, f32[1536]{0:T(1024)S(1)} %copy-done.20, f32[1536]{0:T(1024)S(1)} %copy-done.22, ...), kind=kLoop, calls=%fused_computation.216 | loop fusion | flops 52690944 | bytes 105574400 | tf_op jit(solution)/shard_map/convert.1
  192.3 1.3 multiply_convert_fusion
  193.6 1.1 copy-done.7
  194.7 8.1 %convolution_convert_fusion = bf16[1536,3072]{1,0:T(8,128)(2,1)} fusion(bf16[512,1536]{1,0:T(8,128)(2,1)S(1)} %multiply_convert_fusion, bf16[512,1536]{1,0:T(8,128)(2,1)S(1)} %get-tuple-element.73, bf16[1,512,1536]{2,1,0:T(8,128)(2,1)S(1)} %copy-done.2, f32[1536]{0:T(1024)S(1)} %copy-done.42, f32[512]{0:T(512)S(1)} %copy-done.44, f32[512]{0:T(512)S(1)} %copy-done.27), kind=kOutput, calls=%fused_computation.31 | convolution fusion | flops 4846780416 | bytes 14166016 | tf_op jit(solution)/shard_map/dot_general | solution.py:23
  203.0 0.0 all-reduce.5.cloned.1.call-start
  203.0 8.3 %fusion.47 = (f32[1536]{0:T(1024)S(1)}, f32[1536]{0:T(1024)S(1)}, f32[1536]{0:T(1024)S(1)}, f32[1536]{0:T(1024)S(1)}, f32[1536]{0:T(1024)S(1)}, /*index=5*/f32[1...) fusion(bf16[512,1536]{1,0:T(8,128)(2,1)} %get-tuple-element.80,, ...), kind=kLoop, calls=%fused_computation.85 | loop fusion | flops 29070336 | bytes 58306560 | tf_op jit(solution)/shard_map/reduce_sum | solution.py:71
  211.9 2.8 stack.127
  214.7 0.0 all-reduce.9.cloned.1.call-start
  214.8 92.0 %reduce-scatter.3.cloned.1.call-done = bf16[192,3072]{1,0:T(8,128)(2,1)} async-done(((bf16[1536,3072]{1,0:T(8,128)(2,1)}), bf16[192,3072]{1,0:T(8,128)(2,1)}) %reduce-scatter.3.cloned.1.call-update) | async-done | bytes 1179664 | tf_op jit(solution)/shard_map/reduce_scatter | solution.py:93
  306.8 0.3 all-reduce.7.cloned.1.call-start
  307.1 7.6 %fusion.115 = bf16[1,512,1536]{2,1,0:T(8,128)(2,1)} fusion(bf16[1536,1536]{1,0:T(8,128)(2,1)} %all-gather.5.cloned.1.call-done, bf16[1,512,1536]{2,1,0:T(8,128)(2,1)} %param.7, f32[512,1536]{1,0:T(8,128)} %copy-done.4), kind=kOutput, calls=%fused_computation.224 | convolution fusion | flops 2422210560 | bytes 11010048 | tf_op jit(solution)/shard_map/dot_general | solution.py:57
  314.8 11.1 %fusion.13 = (f32[1536]{0:T(1024)S(1)}, f32[512]{0:T(512)S(1)}, f32[512]{0:T(512)S(1)}, f32[512,1536]{1,0:T(8,128)}) fusion(bf16[1,512,1536]{2,1,0:T(8,128)(2,1)S(1)} %copy-done.3, f32[512]{0:T(512)S(1)} %copy-done.44, f32[512]{0:T(512)S(1)} %copy-done.27, f32[1536]{0:T(1024)S(1)} %copy-done.42, bf16[1536,3072]{1,0:T(8,128)(2,1)} %all-gather.3.cloned.1.call-done, ...), kind=kOutput, calls=%fused_computation.51 | convolution fusion | flops 4845204992 | bytes 17321984 | tf_op jit(solution)/shard_map/dot_general | solution.py:76
  325.9 38.5 %all-reduce.5.cloned.1.call-done = f32[31,1536]{1,0:T(8,128)} async-done(((f32[31,1536]{1,0:T(8,128)}), f32[31,1536]{1,0:T(8,128)}) %all-reduce.5.cloned.1.call-update) | async-done | bytes 190480 | tf_op jit(solution)/shard_map/psum | solution.py:81
  364.4 4.3 fusion.118
  368.7 11.3 %psum.44 = f32[1536]{0:T(1024)S(1)} all-reduce(f32[1536]{0:T(1024)S(1)} %get-tuple-element.37), channel_id=1, replica_groups=mesh['seq'=4,'fsdp'=8] {'fsdp'}, use_global_device_ids=true, to_apply=%region_9.0 | all-reduce | flops 1536 | bytes 12288 | tf_op jit(solution)/shard_map/psum | solution.py:81
  380.0 8.8 %psum.45 = f32[1536]{0:T(1024)} all-reduce(f32[1536]{0:T(1024)S(1)} %psum.44), channel_id=1, replica_groups=mesh['seq'=4,'fsdp'=8] {'seq'}, use_global_device_ids=true, to_apply=%region_10.0 | all-reduce | flops 1536 | bytes 12288 | tf_op jit(solution)/shard_map/psum | solution.py:80
  388.8 43.6 %all-reduce.9.cloned.1.call-done = (bf16[192,3072]{1,0:T(8,128)(2,1)}, bf16[192,1536]{1,0:T(8,128)(2,1)}) async-done(((bf16[192,3072]{1,0:T(8,128)(2,1)}, bf16[192,1536]{1,0:T(8,128)(2,1)}), (bf16[192,3072]{1,0:T(8,128)(2,1)}, bf16[192,1536]{1,0:T(8,128)(2,1)})) %all-reduce.9.cloned.1.call-update) | async-done | bytes 1769488 | tf_op jit(solution)/shard_map/psum | solution.py:101
  432.4 3.0 convert_element_type.88
  435.4 1.1 convert_element_type.90
  436.5 41.5 %all-reduce.7.cloned.1.call-done = f32[31,1536]{1,0:T(8,128)} async-done(((f32[31,1536]{1,0:T(8,128)}), f32[31,1536]{1,0:T(8,128)}) %all-reduce.7.cloned.1.call-update) | async-done | bytes 190480 | tf_op jit(solution)/shard_map/psum | solution.py:80
  478.0 1.6 copy.18
  (137 shorter events, 0.6 us)
Async XLA Ops:
  7.2 4.5 copy-start.12
  7.2 91.9 %copy-start.41 = (f32[1536]{0:T(1024)S(1)}, f32[1536]{0:T(1024)}, u32[]{:S(2)}) copy-start(f32[1536]{0:T(1024)} %param.9) | copy-start | bytes 18436
  7.2 91.9 %all-gather.3.cloned.1.call-start = ((), (), s32[]{:S(2)}) async-start(), calls=%async_computation.2 | async-start | bytes 10616832 | tf_op jit(solution)/shard_map/all_gather | solution.py:36
  7.9 144.0 %all-gather.5.cloned.1.call-start = ((), (), s32[]{:S(2)}) async-start(), calls=%async_computation.3 | async-start | bytes 5308416 | tf_op jit(solution)/shard_map/all_gather | solution.py:37
  8.7 206.1 %reduce-scatter.5.cloned.1.call-start = ((), (), s32[]{:S(2)}) async-start(), calls=%async_computation.5 | async-start | bytes 5308416 | tf_op jit(solution)/shard_map/reduce_scatter | solution.py:96
  11.1 95.6 %copy-start.26 = (f32[512]{0:T(512)}, f32[512]{0:T(512)S(1)}, u32[]{:S(2)}) copy-start(f32[512]{0:T(512)S(1)} %broadcast_multiply_fusion.2) | copy-start | bytes 6148
  11.7 95.1 %copy-start.43 = (f32[512]{0:T(512)}, f32[512]{0:T(512)S(1)}, u32[]{:S(2)}) copy-start(f32[512]{0:T(512)S(1)} %add_rsqrt_fusion) | copy-start | bytes 6148
  12.0 94.7 %copy-start.23 = (f32[512]{0:T(512)}, f32[512]{0:T(512)S(1)}, u32[]{:S(2)}) copy-start(f32[512]{0:T(512)S(1)} %fusion.121) | copy-start | bytes 6148
  109.5 6.1 %collective-permute-start = (bf16[1,15,1536]{2,1,0:T(8,128)(2,1)S(1)}, bf16[1,15,1536]{2,1,0:T(8,128)(2,1)S(1)}, u32[]{:S(2)}, u32[]{:S(2)}) collective-permute-start(bf16[1,15,1536]{2,1,0:T(8,128)(2,1)S(1)} %get-tuple-element.77), channel_id=1, source_target_pairs={{0,8},{8,16},{16,24},{1,9},{9,17},{17,25},{2,10},{10,18},{18,26},{... | collective-permute-start | bytes 138248 | tf_op jit(solution)/shard_map/ppermute | solution.py:14
  112.9 6.9 %collective-permute-start.1 = (bf16[1,15,1536]{2,1,0:T(8,128)(2,1)S(1)}, bf16[1,15,1536]{2,1,0:T(8,128)(2,1)S(1)}, u32[]{:S(2)}, u32[]{:S(2)}) collective-permute-start(bf16[1,15,1536]{2,1,0:T(8,128)(2,1)S(1)} %get-tuple-element.78), channel_id=1, source_target_pairs={{8,0},{16,8},{24,16},{9,1},{17,9},{25,17},{10,2},{18,10},{26,18},{... | collective-permute-start | bytes 138248 | tf_op jit(solution)/shard_map/ppermute | solution.py:17
  115.5 16.7 %copy-start.13 = (f32[1536]{0:T(1024)}, f32[1536]{0:T(1024)S(1)}, u32[]{:S(2)}) copy-start(f32[1536]{0:T(1024)S(1)} %get-tuple-element.66) | copy-start | bytes 18436
  115.5 16.7 %copy-start.15 = (f32[1536]{0:T(1024)}, f32[1536]{0:T(1024)S(1)}, u32[]{:S(2)}) copy-start(f32[1536]{0:T(1024)S(1)} %get-tuple-element.67) | copy-start | bytes 18436
  115.5 16.7 %copy-start.17 = (f32[1536]{0:T(1024)}, f32[1536]{0:T(1024)S(1)}, u32[]{:S(2)}) copy-start(f32[1536]{0:T(1024)S(1)} %get-tuple-element.68) | copy-start | bytes 18436
  115.6 16.7 %copy-start.19 = (f32[1536]{0:T(1024)}, f32[1536]{0:T(1024)S(1)}, u32[]{:S(2)}) copy-start(f32[1536]{0:T(1024)S(1)} %get-tuple-element.69) | copy-start | bytes 18436
  115.6 16.7 %copy-start.21 = (f32[1536]{0:T(1024)}, f32[1536]{0:T(1024)S(1)}, u32[]{:S(2)}) copy-start(f32[1536]{0:T(1024)S(1)} %get-tuple-element.70) | copy-start | bytes 18436
  120.2 13.8 %copy-start.5 = (bf16[1,512,1536]{2,1,0:T(8,128)(2,1)S(1)}, bf16[1,512,1536]{2,1,0:T(8,128)(2,1)}, u32[]{:S(2)}) copy-start(bf16[1,512,1536]{2,1,0:T(8,128)(2,1)} %param.13) | copy-start | bytes 4718596
  120.2 13.8 %copy-start.24 = (f32[512]{0:T(512)S(1)}, f32[512]{0:T(512)}, u32[]{:S(2)}) copy-start(f32[512]{0:T(512)} %copy-done.23) | copy-start | bytes 6148
  138.9 167.9 %reduce-scatter.3.cloned.1.call-start = ((), (), s32[]{:S(2)}) async-start(), calls=%async_computation.4 | async-start | bytes 10616832 | tf_op jit(solution)/shard_map/reduce_scatter | solution.py:93
  164.5 13.3 %copy-start.14 = (f32[1536]{0:T(1024)S(1)}, f32[1536]{0:T(1024)}, u32[]{:S(2)}) copy-start(f32[1536]{0:T(1024)} %copy-done.13) | copy-start | bytes 18436
  164.5 13.3 %copy-start.16 = (f32[1536]{0:T(1024)S(1)}, f32[1536]{0:T(1024)}, u32[]{:S(2)}) copy-start(f32[1536]{0:T(1024)} %copy-done.15) | copy-start | bytes 18436
  164.5 13.3 %copy-start.18 = (f32[1536]{0:T(1024)S(1)}, f32[1536]{0:T(1024)}, u32[]{:S(2)}) copy-start(f32[1536]{0:T(1024)} %copy-done.17) | copy-start | bytes 18436
  164.5 13.3 %copy-start.20 = (f32[1536]{0:T(1024)S(1)}, f32[1536]{0:T(1024)}, u32[]{:S(2)}) copy-start(f32[1536]{0:T(1024)} %copy-done.19) | copy-start | bytes 18436
  164.5 13.3 %copy-start.22 = (f32[1536]{0:T(1024)S(1)}, f32[1536]{0:T(1024)}, u32[]{:S(2)}) copy-start(f32[1536]{0:T(1024)} %copy-done.21) | copy-start | bytes 18436
  164.5 13.3 %copy-start.25 = (f32[512]{0:T(512)S(1)}, f32[512]{0:T(512)}, u32[]{:S(2)}) copy-start(f32[512]{0:T(512)} %copy-done.23) | copy-start | bytes 6148
  165.4 6.0 %collective-permute-start.2 = (bf16[1,15,1536]{2,1,0:T(8,128)(2,1)S(1)}, bf16[1,15,1536]{2,1,0:T(8,128)(2,1)S(1)}, u32[]{:S(2)}, u32[]{:S(2)}) collective-permute-start(bf16[1,15,1536]{2,1,0:T(8,128)(2,1)S(1)} %get-tuple-element.75), channel_id=1, source_target_pairs={{0,8},{8,16},{16,24},{1,9},{9,17},{17,25},{2,10},{10,18},{18,26},{... | collective-permute-start | bytes 138248 | tf_op jit(solution)/shard_map/ppermute | solution.py:14
  168.8 6.9 %collective-permute-start.3 = (bf16[1,15,1536]{2,1,0:T(8,128)(2,1)S(1)}, bf16[1,15,1536]{2,1,0:T(8,128)(2,1)S(1)}, u32[]{:S(2)}, u32[]{:S(2)}) collective-permute-start(bf16[1,15,1536]{2,1,0:T(8,128)(2,1)S(1)} %get-tuple-element.76), channel_id=1, source_target_pairs={{8,0},{16,8},{24,16},{9,1},{17,9},{25,17},{10,2},{18,10},{26,18},{... | collective-permute-start | bytes 138248 | tf_op jit(solution)/shard_map/ppermute | solution.py:17
  175.7 16.5 %slice-start = ((s8[6291456]{0:T(1024)(128)(4,1)}), s8[4194304]{0:T(1024)(128)(4,1)S(1)}, s32[]{:S(2)}) async-start(s8[6291456]{0:T(1024)(128)(4,1)} %bitcast.526), calls=%async_computation.9 | async-start | bytes 8388608
  177.8 14.4 %slice-start.1 = ((s8[6291456]{0:T(1024)(128)(4,1)}), s8[2097152]{0:T(1024)(128)(4,1)S(1)}, s32[]{:S(2)}) async-start(s8[6291456]{0:T(1024)(128)(4,1)} %bitcast.526), calls=%async_computation.10 | async-start | bytes 4194304
  202.8 8.5 %copy-start.40 = (f32[1536]{0:T(1024)S(1)}, f32[1536]{0:T(1024)}, u32[]{:S(2)}) copy-start(f32[1536]{0:T(1024)} %get-tuple-element.24) | copy-start | bytes 18436
  202.8 8.6 %copy-start.39 = (f32[1536]{0:T(1024)S(1)}, f32[1536]{0:T(1024)}, u32[]{:S(2)}) copy-start(f32[1536]{0:T(1024)} %get-tuple-element.25) | copy-start | bytes 18436
  202.8 8.6 %copy-start.38 = (f32[1536]{0:T(1024)S(1)}, f32[1536]{0:T(1024)}, u32[]{:S(2)}) copy-start(f32[1536]{0:T(1024)} %get-tuple-element.26) | copy-start | bytes 18436
  202.9 8.6 %copy-start.37 = (f32[1536]{0:T(1024)S(1)}, f32[1536]{0:T(1024)}, u32[]{:S(2)}) copy-start(f32[1536]{0:T(1024)} %get-tuple-element.27) | copy-start | bytes 18436
  202.9 8.6 %copy-start.36 = (f32[1536]{0:T(1024)S(1)}, f32[1536]{0:T(1024)}, u32[]{:S(2)}) copy-start(f32[1536]{0:T(1024)} %get-tuple-element.28) | copy-start | bytes 18436
  202.9 8.6 %copy-start.35 = (f32[1536]{0:T(1024)S(1)}, f32[1536]{0:T(1024)}, u32[]{:S(2)}) copy-start(f32[1536]{0:T(1024)} %get-tuple-element.29) | copy-start | bytes 18436
  202.9 8.6 %copy-start.34 = (f32[1536]{0:T(1024)S(1)}, f32[1536]{0:T(1024)}, u32[]{:S(2)}) copy-start(f32[1536]{0:T(1024)} %get-tuple-element.30) | copy-start | bytes 18436
  202.9 8.6 %copy-start.33 = (f32[1536]{0:T(1024)S(1)}, f32[1536]{0:T(1024)}, u32[]{:S(2)}) copy-start(f32[1536]{0:T(1024)} %get-tuple-element.31) | copy-start | bytes 18436
  202.9 8.6 %copy-start.32 = (f32[1536]{0:T(1024)S(1)}, f32[1536]{0:T(1024)}, u32[]{:S(2)}) copy-start(f32[1536]{0:T(1024)} %get-tuple-element.32) | copy-start | bytes 18436
  202.9 8.7 %copy-start.31 = (f32[1536]{0:T(1024)S(1)}, f32[1536]{0:T(1024)}, u32[]{:S(2)}) copy-start(f32[1536]{0:T(1024)} %get-tuple-element.33) | copy-start | bytes 18436
  202.9 8.7 %copy-start.30 = (f32[1536]{0:T(1024)S(1)}, f32[1536]{0:T(1024)}, u32[]{:S(2)}) copy-start(f32[1536]{0:T(1024)} %get-tuple-element.34) | copy-start | bytes 18436
  202.9 8.7 %copy-start.29 = (f32[1536]{0:T(1024)S(1)}, f32[1536]{0:T(1024)}, u32[]{:S(2)}) copy-start(f32[1536]{0:T(1024)} %get-tuple-element.35) | copy-start | bytes 18436
  202.9 8.7 %copy-start.28 = (f32[1536]{0:T(1024)S(1)}, f32[1536]{0:T(1024)}, u32[]{:S(2)}) copy-start(f32[1536]{0:T(1024)} %get-tuple-element.36) | copy-start | bytes 18436
  203.0 161.4 %all-reduce.5.cloned.1.call-start = ((), (), s32[]{:S(2)}) async-start(), calls=%async_computation.6 | async-start | bytes 393216 | tf_op jit(solution)/shard_map/psum | solution.py:81
  214.7 217.7 %all-reduce.9.cloned.1.call-start = ((), (), s32[]{:S(2)}) async-start(), calls=%async_computation.8 | async-start | bytes 3538944 | tf_op jit(solution)/shard_map/psum | solution.py:101
  306.8 7.9 %copy-start.3 = (bf16[1,512,1536]{2,1,0:T(8,128)(2,1)S(1)}, bf16[1,512,1536]{2,1,0:T(8,128)(2,1)}, u32[]{:S(2)}) copy-start(bf16[1,512,1536]{2,1,0:T(8,128)(2,1)} %param.7) | copy-start | bytes 4718596
  306.8 171.2 %all-reduce.7.cloned.1.call-start = ((), (), s32[]{:S(2)}) async-start(), calls=%async_computation.7 | async-start | bytes 393216 | tf_op jit(solution)/shard_map/psum | solution.py:80
  307.1 7.7 %copy-start.8 = (bf16[512,1536]{1,0:T(8,128)(2,1)S(1)}, bf16[512,1536]{1,0:T(8,128)(2,1)}, u32[]{:S(2)}) copy-start(bf16[512,1536]{1,0:T(8,128)(2,1)} %copy-done.7) | copy-start | bytes 4718596
  307.1 7.7 %copy-start.10 = (bf16[512,1536]{1,0:T(8,128)(2,1)S(1)}, bf16[512,1536]{1,0:T(8,128)(2,1)}, u32[]{:S(2)}) copy-start(bf16[512,1536]{1,0:T(8,128)(2,1)} %copy-done.9) | copy-start | bytes 4718596
  314.8 49.6 %copy-start.6 = (bf16[1,512,1536]{2,1,0:T(8,128)(2,1)S(1)}, bf16[1,512,1536]{2,1,0:T(8,128)(2,1)}, u32[]{:S(2)}) copy-start(bf16[1,512,1536]{2,1,0:T(8,128)(2,1)} %param.13) | copy-start | bytes 4718596
  (10 other events, 23.8 us)
Sparse Core Ops, SparseCore 0:
  9.7 89.3 all-gather.2
  100.7 51.1 all-gather.4
  154.2 52.4 reduce-scatter.4
  208.9 97.8 reduce-scatter.2
  309.5 54.7 all-reduce.4
  367.8 64.5 all-reduce.8
  435.5 42.4 all-reduce.6
